TPU v7x, 256 devices: a whole 4x4x8 slice. The times are simulated.
256 devices in a mesh: slab: 4 (over y_hi, core), row: 8 (over x, y_lo), col: 8 (over z).
Axes of the slice: x: 4, y: 4 (y_hi: 2, y_lo: 2; y = y_hi * 2 + y_lo), z: 8, core: 2. Of those that a mesh axis runs over, the one named last changes fastest.
Arguments:
- reflection: bfloat16 [4, 4096, 4096], P('slab', 'row', 'col'), may hold values from -0.0625 to 0.0625
- transmission: bfloat16 [4, 4096, 4096], P('slab', 'row', 'col'), may hold values from -0.09375 to 0.09375
- shots: bfloat16 [4, 4096, 2048], P('slab', 'row', 'col'), may hold values from -6 to 6
Outputs:
- merged: bfloat16 [4, 4096, 2048], P('slab', 'row', 'col')
All inputs are finite; a program needn't handle non-finite values.
Results may differ from a plain program's by a relative error of at most 0.008.
Values may be sent and summed in bfloat16 or wider, within the bound.
No kernel may reach another device: no remote copies, remote signals or barrier semaphores. Data moves between devices by JAX's collectives and lax.ppermute only.
A program may use at most 64 MiB of HBM per device.

v0:
```python
import jax
import jax.numpy as jnp
from jax import lax
from jax.sharding import PartitionSpec as P


def partner(block, axis, bit):
    count = lax.axis_size(axis)
    route = []
    for low in range(count):
        high = low | 1 << bit
        if high != low and high < count:
            route += [(low, high), (high, low)]
    return lax.ppermute(block, axis, route)


def in_order(parts, dim):
    parts = jnp.moveaxis(parts, 0, dim)
    dims = parts.shape
    return parts.reshape(*dims[:dim], dims[dim] * dims[dim + 1], *dims[dim + 2 :])


def from_everyone(array, axis):
    copies = jnp.broadcast_to(array, (lax.axis_size(axis), *array.shape))
    return lax.all_to_all(copies, axis, split_axis=0, concat_axis=0, tiled=True)


def collect(array, axis, dim):
    return in_order(from_everyone(array, axis), dim)


def fold_with(panel, highest, piece):
    if highest:
        return jnp.dot(
            panel.astype(jnp.float32), piece.astype(jnp.float32), precision=lax.Precision.HIGHEST
        )
    return jnp.dot(panel, piece, preferred_element_type=jnp.float32)


def on_device(reflection, transmission, shots):
    own_refl = reflection[0]
    own_trans = transmission[0]
    shot_tile = shots[0]
    far_refl, far_trans = partner((own_refl, own_trans), "slab", 0)
    trans_panel = lax.all_gather(own_trans, "col", axis=1, tiled=True)
    first = fold_with(trans_panel, False, collect(shot_tile, "row", 0)).astype(jnp.bfloat16)
    partner_panel = lax.all_gather(far_refl, "col", axis=1, tiled=True)
    middle = fold_with(partner_panel, False, collect(first, "row", 0))
    own_panel = lax.all_gather(own_refl, "col", axis=1, tiled=True)
    bounce = fold_with(
        own_panel,
        True,
        lax.all_gather(middle.astype(jnp.bfloat16), "row", axis=0, tiled=True).astype(jnp.float32),
    )
    summed = (first.astype(jnp.float32) + bounce).astype(jnp.bfloat16)
    out_panel = lax.all_gather(far_trans, "col", axis=1, tiled=True)
    merged = fold_with(out_panel, False, collect(summed, "row", 0))
    return merged.astype(jnp.bfloat16)[None]


def solution(mesh):
    placed = (P("slab", "row", "col"), P("slab", "row", "col"), P("slab", "row", "col"))
    return jax.shard_map(
        on_device, mesh=mesh, in_specs=placed, out_specs=P("slab", "row", "col"), check_vma=False
    )
```

profile of v0, /device:TPU:1, one launch (start us, length us, event | category | flops | bytes accessed | tf_op | source)
XLA Modules:
  0.0 299.9 jit_solution(3459101234463216938)
XLA Ops:
  6.5 0.0 all-gather.14.cloned.1.call-start
  6.5 0.7 all-gather.14.cloned.1.call-update
  7.3 0.0 all-gather.8.cloned.1.call-start
  7.3 3.3 %collective-permute-start = (bf16[512,512]{1,0:T(8,128)(2,1)}, bf16[512,512]{1,0:T(8,128)(2,1)S(1)}, u32[]{:S(2)}, u32[]{:S(2)}) collective-permute-start(bf16[512,512]{1,0:T(8,128)(2,1)} %bitcast.42), channel_id=1, source_target_pairs={{0,64},{64,0},{128,192},{192,128},{1,65},{65,1},{129,193},{193,129... | collective-permute-start | bytes 1572872 | tf_op jit(solution)/shard_map/ppermute | solution.py:14
  10.6 1.7 collective-permute-done
  12.4 0.0 copy-start.1
  12.4 0.8 copy-done.1
  13.2 0.0 all-gather.8.cloned.1.call-update
  13.3 0.0 all-gather.16.cloned.1.call-start
  13.3 0.7 all-gather.16.cloned.1.call-update
  14.0 1.1 broadcast_in_dim.12
  15.1 28.6 %all_to_all.15 = bf16[8,512,256]{2,1,0:T(8,128)(2,1)S(1)} all-to-all(bf16[8,512,256]{2,1,0:T(8,128)(2,1)S(1)} %broadcast_in_dim.12), channel_id=1, replica_groups=mesh['slab'=4,'row'=8,'col'=8] {'row'}, dimensions={0} | all-to-all | bytes 4194304 | tf_op jit(solution)/shard_map/all_to_all | solution.py:25
  43.7 24.1 %all-gather.14.cloned.1.call-done = bf16[1,512,4096]{2,1,0:T(8,128)(2,1)} async-done(((bf16[1,512,512]{2,1,0:T(8,128)(2,1)}), bf16[1,512,4096]{2,1,0:T(8,128)(2,1)}) %all-gather.14.cloned.1.call-update) | async-done | bytes 4194320 | tf_op jit(solution)/shard_map/all_gather | solution.py:45
  67.8 3.4 %fusion.13 = bf16[512,256]{1,0:T(8,128)(2,1)S(1)} fusion(bf16[4096,256]{1,0:T(8,128)(2,1)S(1)} %bitcast.40, bf16[1,512,4096]{2,1,0:T(8,128)(2,1)} %all-gather.14.cloned.1.call-done), kind=kOutput, calls=%fused_computation.7 | convolution fusion | flops 1073872896 | bytes 6553600 | tf_op jit(solution)/shard_map/dot_general | solution.py:37
  71.2 1.5 broadcast_in_dim.13
  72.8 4.9 %all-to-all-start.1 = ((bf16[8,512,256]{2,1,0:T(8,128)(2,1)}), bf16[8,512,256]{2,1,0:T(8,128)(2,1)S(1)}, u32[]{:S(2)}, u32[]{:S(2)}) async-start(bf16[8,512,256]{2,1,0:T(8,128)(2,1)} %broadcast_in_dim.13), calls=%async_computation.1 | async-start | bytes 4194304 | tf_op jit(solution)/shard_map/all_to_all | solution.py:25
  77.7 0.0 all-gather.10.cloned.1.call-start
  77.7 45.3 %all-gather.8.cloned.1.call-done = bf16[512,4096]{1,0:T(8,128)(2,1)} async-done(((bf16[512,512]{1,0:T(8,128)(2,1)}), bf16[512,4096]{1,0:T(8,128)(2,1)}) %all-gather.8.cloned.1.call-update) | async-done | bytes 4194320 | tf_op jit(solution)/shard_map/all_gather | solution.py:47
  123.1 0.0 all-to-all-done.1
  123.1 0.0 copy-start
  123.1 4.2 %fusion.16 = bf16[512,256]{0,1:T(8,128)(2,1)} fusion(bf16[4096,256]{1,0:T(8,128)(2,1)S(1)} %bitcast.38, bf16[512,4096]{1,0:T(8,128)(2,1)} %all-gather.8.cloned.1.call-done), kind=kOutput, calls=%fused_computation.10 | convolution fusion | flops 1073872896 | bytes 6553600 | tf_op jit(solution)/shard_map/dot_general | solution.py:37
  127.3 0.0 all-gather.10.cloned.1.call-update
  127.3 0.0 all-gather.12.cloned.1.call-start
  127.4 0.0 copy-done
  127.4 0.8 collective-permute-start.1
  128.2 1.5 collective-permute-done.1
  129.7 0.0 copy-start.2
  129.7 0.8 copy-done.2
  130.5 0.0 all-gather.12.cloned.1.call-update
  130.5 47.8 %all-gather.16.cloned.1.call-done = bf16[1,512,4096]{2,1,0:T(8,128)(2,1)} async-done(((bf16[1,512,512]{2,1,0:T(8,128)(2,1)}), bf16[1,512,4096]{2,1,0:T(8,128)(2,1)}) %all-gather.16.cloned.1.call-update) | async-done | bytes 4194320 | tf_op jit(solution)/shard_map/all_gather | solution.py:49
  178.3 53.4 %all-gather.10.cloned.1.call-done = bf16[4096,256]{0,1:T(8,128)(2,1)} async-done(((bf16[512,256]{0,1:T(8,128)(2,1)}), bf16[4096,256]{0,1:T(8,128)(2,1)}) %all-gather.10.cloned.1.call-update) | async-done | bytes 2097168 | tf_op jit(solution)/shard_map/all_gather | solution.py:53
  231.7 4.1 %fusion.10 = bf16[512,256]{1,0:T(8,128)(2,1)S(1)} fusion(bf16[4096,256]{0,1:T(8,128)(2,1)} %all-gather.10.cloned.1.call-done, bf16[1,512,4096]{2,1,0:T(8,128)(2,1)} %all-gather.16.cloned.1.call-done, bf16[512,256]{1,0:T(8,128)(2,1)S(1)} %fusion.13), kind=kOutput, calls=%fused_computation.6 | convolution fusion | flops 1074135040 | bytes 6815744 | tf_op jit(solution)/shard_map/dot_general | solution.py:34
  235.8 1.5 broadcast_in_dim.14
  237.3 4.5 %all-to-all-start.2 = ((bf16[8,512,256]{2,1,0:T(8,128)(2,1)}), bf16[8,512,256]{2,1,0:T(8,128)(2,1)S(1)}, u32[]{:S(2)}, u32[]{:S(2)}) async-start(bf16[8,512,256]{2,1,0:T(8,128)(2,1)} %broadcast_in_dim.14), calls=%async_computation.2 | async-start | bytes 4194304 | tf_op jit(solution)/shard_map/all_to_all | solution.py:25
  241.8 47.3 %all-gather.12.cloned.1.call-done = bf16[512,4096]{1,0:T(8,128)(2,1)} async-done(((bf16[512,512]{1,0:T(8,128)(2,1)}), bf16[512,4096]{1,0:T(8,128)(2,1)}) %all-gather.12.cloned.1.call-update) | async-done | bytes 4194320 | tf_op jit(solution)/shard_map/all_gather | solution.py:56
  289.0 0.0 all-to-all-done.2
  289.0 3.5 %fusion.17 = bf16[1,512,256]{1,2,0:T(8,128)(2,1)S(1)} fusion(bf16[4096,256]{1,0:T(8,128)(2,1)S(1)} %bitcast.39, bf16[512,4096]{1,0:T(8,128)(2,1)} %all-gather.12.cloned.1.call-done), kind=kOutput, calls=%fused_computation.11 | convolution fusion | flops 1073872896 | bytes 6553600 | tf_op jit(solution)/shard_map/dot_general | solution.py:37
  292.5 0.8 copy.5
Async XLA Ops:
  6.5 61.3 %all-gather.14.cloned.1.call-start = ((), (), s32[]{:S(2)}) async-start(), calls=%async_computation.6 | async-start | bytes 4718592 | tf_op jit(solution)/shard_map/all_gather | solution.py:45
  7.3 115.8 %all-gather.8.cloned.1.call-start = ((), (), s32[]{:S(2)}) async-start(), calls=%async_computation.3 | async-start | bytes 4718592 | tf_op jit(solution)/shard_map/all_gather | solution.py:47
  7.3 5.1 %collective-permute-start = (bf16[512,512]{1,0:T(8,128)(2,1)}, bf16[512,512]{1,0:T(8,128)(2,1)S(1)}, u32[]{:S(2)}, u32[]{:S(2)}) collective-permute-start(bf16[512,512]{1,0:T(8,128)(2,1)} %bitcast.42), channel_id=1, source_target_pairs={{0,64},{64,0},{128,192},{192,128},{1,65},{65,1},{129,193},{193,129... | collective-permute-start | bytes 1572872 | tf_op jit(solution)/shard_map/ppermute | solution.py:14
  12.4 0.9 copy-start.1
  13.3 165.1 %all-gather.16.cloned.1.call-start = ((), (), s32[]{:S(2)}) async-start(), calls=%async_computation.7 | async-start | bytes 4718592 | tf_op jit(solution)/shard_map/all_gather | solution.py:49
  72.8 50.3 %all-to-all-start.1 = ((bf16[8,512,256]{2,1,0:T(8,128)(2,1)}), bf16[8,512,256]{2,1,0:T(8,128)(2,1)S(1)}, u32[]{:S(2)}, u32[]{:S(2)}) async-start(bf16[8,512,256]{2,1,0:T(8,128)(2,1)} %broadcast_in_dim.13), calls=%async_computation.1 | async-start | bytes 4194304 | tf_op jit(solution)/shard_map/all_to_all | solution.py:25
  77.7 154.0 %all-gather.10.cloned.1.call-start = ((), (), s32[]{:S(2)}) async-start(), calls=%async_computation.4 | async-start | bytes 2359296 | tf_op jit(solution)/shard_map/all_gather | solution.py:53
  123.1 4.3 %copy-start = (bf16[1,512,512]{2,1,0:T(8,128)(2,1)S(1)}, bf16[1,512,512]{2,1,0:T(8,128)(2,1)}, u32[]{:S(2)}) copy-start(bf16[1,512,512]{2,1,0:T(8,128)(2,1)} %param.4) | copy-start | bytes 1572868
  127.3 161.7 %all-gather.12.cloned.1.call-start = ((), (), s32[]{:S(2)}) async-start(), calls=%async_computation.5 | async-start | bytes 4718592 | tf_op jit(solution)/shard_map/all_gather | solution.py:56
  127.4 2.3 collective-permute-start.1
  129.7 0.8 copy-start.2
  237.3 51.8 %all-to-all-start.2 = ((bf16[8,512,256]{2,1,0:T(8,128)(2,1)}), bf16[8,512,256]{2,1,0:T(8,128)(2,1)S(1)}, u32[]{:S(2)}, u32[]{:S(2)}) async-start(bf16[8,512,256]{2,1,0:T(8,128)(2,1)} %broadcast_in_dim.14), calls=%async_computation.2 | async-start | bytes 4194304 | tf_op jit(solution)/shard_map/all_to_all | solution.py:25
Sparse Core Ops, SparseCore 0:
  9.1 58.6 all-gather.13
  69.6 53.4 all-gather.7
  124.9 53.4 all-gather.15
  180.0 51.6 all-gather.9
  233.3 55.6 all-gather.11
where the time goes:
time: 300 us
  waiting for transfers between devices  223 us (74%)
  blocking collectives  28.6 us (10%)
  matrix products  15.3 us (5%)
  starting transfers between devices  13.7 us (5%)
  between operations  13.2 us (4%)
  local copies, waits for them, and re-layouts  6.57 us (2%)
    all_gather x1, waiting for transfers between devices, on_device(): lax.all_gather(middle.astype(jnp.bfloat16), 'row', axis=0, tiled=True)  53.4 us
    all_gather x1, waiting for transfers between devices, on_device(): own_panel = lax.all_gather(own_refl, 'col', axis=1, tiled=True)  47.8 us
    all_gather x1, waiting for transfers between devices, on_device(): out_panel = lax.all_gather(far_trans, 'col', axis=1, tiled=True)  47.3 us
    all_gather x1, waiting for transfers between devices, on_device(): partner_panel = lax.all_gather(far_refl, 'col', axis=1, tiled=True)  45.3 us
    all_to_all x1, blocking collectives, from_everyone(): return lax.all_to_all(copies, axis, split_axis=0, concat_axis=0, tiled=True)  28.6 us
    all_gather x1, waiting for transfers between devices, on_device(): trans_panel = lax.all_gather(own_trans, 'col', axis=1, tiled=True)  24.1 us
    dot_general x3, matrix products, fold_with(): return jnp.dot(panel, piece, preferred_element_type=jnp.float32)  11.2 us
    all_to_all x2, starting transfers between devices, from_everyone(): return lax.all_to_all(copies, axis, split_axis=0, concat_axis=0, tiled=True)  9.41 us
  transfers between devices with their start and end apart: 9, of which 7 were waited for; matrix products, arithmetic and copies ran while one was open for 5% of the time, Pallas kernels for 0%

commit v1 on v0

--- a/solution.py
+++ b/solution.py
@@ -46,7 +46,21 @@
     first = fold_with(trans_panel, False, collect(shot_tile, "row", 0)).astype(jnp.bfloat16)
     partner_panel = lax.all_gather(far_refl, "col", axis=1, tiled=True)
     middle = fold_with(partner_panel, False, collect(first, "row", 0))
-    own_panel = lax.all_gather(own_refl, "col", axis=1, tiled=True)
+    ways, here, hop = (lax.axis_size("col"), lax.axis_index("col"), own_refl.shape[1])
+    lengths = [n * ways if d == 1 else n for d, n in enumerate(own_refl.shape)]
+    full = lax.dynamic_update_slice_in_dim(
+        jnp.zeros(lengths, own_refl.dtype), own_refl, here * hop, axis=1
+    )
+    going_up = going_down = own_refl
+    for far in range(1, ways // 2 + 1):
+        going_up = lax.ppermute(going_up, "col", [(d, (d + 1) % ways) for d in range(ways)])
+        full = lax.dynamic_update_slice_in_dim(full, going_up, (here - far) % ways * hop, axis=1)
+        if 2 * far < ways:
+            going_down = lax.ppermute(going_down, "col", [(d, (d - 1) % ways) for d in range(ways)])
+            full = lax.dynamic_update_slice_in_dim(
+                full, going_down, (here + far) % ways * hop, axis=1
+            )
+    own_panel = full
     bounce = fold_with(
         own_panel,
         True,

time: 300 us -> 248 us (0.83)
  waiting for transfers between devices: 223 us -> 151 us
  local copies, waits for them, and re-layouts: 6.57 us -> 16.3 us
  starting transfers between devices: 13.7 us -> 22.6 us
    all_gather x1, waiting for transfers between devices: 53.4 us -> 0.01 us  [on_device(): lax.all_gather(middle.astype(jnp.bfloat16), 'row', axis=0, tiled=True)]
    all_gather x1 -> x0, waiting for transfers between devices: 47.8 us -> none  [on_device(): own_panel = lax.all_gather(own_refl, 'col', axis=1, tiled=True)]
    ppermute x0 -> x7, waiting for transfers between devices: none -> 35.2 us  [the longest x4 35.2 us: on_device(): lax.ppermute(going_up, 'col', [(d, (d + 1) % ways) for d in range(ways)])]
    ppermute x0 -> x7, starting transfers between devices: none -> 8.12 us  [the longest x3 8.03 us: on_device(): lax.ppermute(going_down, 'col', [(d, (d - 1) % ways) for d in range(ways)])]
    dynamic_update_slice x0 -> x8, local copies, waits for them, and re-layouts: none -> 7.17 us  [the longest x4 3.7 us: on_device(): lax.dynamic_update_slice_in_dim(full, going_up, (here - far) % ways * hop...]
    all_gather x1, waiting for transfers between devices: 47.3 us -> 42 us  [on_device(): out_panel = lax.all_gather(far_trans, 'col', axis=1, tiled=True)]
  transfers between devices with their start and end apart: 9 -> 15, of which waited for: 7 -> 9; matrix products, arithmetic and copies ran while one was open for 5% -> 9% of each run, Pallas kernels for 0% -> 0%
where the time goes in v1:
time: 248 us; the launch traced here: 247 us
  waiting for transfers between devices  151 us (61%)
  blocking collectives  28.6 us (12%)
  starting transfers between devices  22.6 us (9%)
  local copies, waits for them, and re-layouts  16.3 us (7%)
  matrix products  15.3 us (6%)
  between operations  13.2 us (5%)
    all_gather x1, waiting for transfers between devices, on_device(): partner_panel = lax.all_gather(far_refl, 'col', axis=1, tiled=True)  45.4 us
    all_gather x1, waiting for transfers between devices, on_device(): out_panel = lax.all_gather(far_trans, 'col', axis=1, tiled=True)  42 us
    ppermute x4, waiting for transfers between devices, on_device(): lax.ppermute(going_up, 'col', [(d, (d + 1) % ways) for d in range(ways)])  35.2 us
    all_to_all x1, blocking collectives, from_everyone(): return lax.all_to_all(copies, axis, split_axis=0, concat_axis=0, tiled=True)  28.6 us
    all_gather x1, waiting for transfers between devices, on_device(): trans_panel = lax.all_gather(own_trans, 'col', axis=1, tiled=True)  24.8 us
    dot_general x3, matrix products, fold_with(): return jnp.dot(panel, piece, preferred_element_type=jnp.float32)  11.2 us
    all_to_all x2, starting transfers between devices, from_everyone(): return lax.all_to_all(copies, axis, split_axis=0, concat_axis=0, tiled=True)  10.2 us
    ppermute x3, starting transfers between devices, on_device(): lax.ppermute(going_down, 'col', [(d, (d - 1) % ways) for d in range(ways)])  8.03 us
  transfers between devices with their start and end apart: 15, of which 9 were waited for; matrix products, arithmetic and copies ran while one was open for 9% of the time, Pallas kernels for 0%

profile of v1, /device:TPU:1, one launch (start us, length us, event | category | flops | bytes accessed | tf_op | source)
XLA Modules:
  0.0 247.4 jit_solution(2766846508178069135)
XLA Ops:
  6.5 0.7 all-gather.12.cloned.1.call-update
  7.3 0.0 all-gather.6.cloned.1.call-start
  7.3 3.3 %collective-permute-start.7 = (bf16[512,512]{1,0:T(8,128)(2,1)}, bf16[512,512]{1,0:T(8,128)(2,1)S(1)}, u32[]{:S(2)}, u32[]{:S(2)}) collective-permute-start(bf16[512,512]{1,0:T(8,128)(2,1)} %bitcast.29), channel_id=1, source_target_pairs={{0,64},{64,0},{128,192},{192,128},{1,65},{65,1},{129,193},{193,129... | collective-permute-start | bytes 1572872 | tf_op jit(solution)/shard_map/ppermute | solution.py:14
  10.6 1.7 collective-permute-done.7
  12.4 0.9 copy-done.2
  13.2 0.0 all-gather.6.cloned.1.call-update
  13.3 1.1 broadcast_in_dim.15
  14.4 28.6 %all_to_all.15 = bf16[8,512,256]{2,1,0:T(8,128)(2,1)S(1)} all-to-all(bf16[8,512,256]{2,1,0:T(8,128)(2,1)S(1)} %broadcast_in_dim.15), channel_id=1, replica_groups=mesh['slab'=4,'row'=8,'col'=8] {'row'}, dimensions={0} | all-to-all | bytes 4194304 | tf_op jit(solution)/shard_map/all_to_all | solution.py:25
  43.0 24.8 %all-gather.12.cloned.1.call-done = bf16[1,512,4096]{2,1,0:T(8,128)(2,1)} async-done(((bf16[1,512,512]{2,1,0:T(8,128)(2,1)}), bf16[1,512,4096]{2,1,0:T(8,128)(2,1)}) %all-gather.12.cloned.1.call-update) | async-done | bytes 4194320 | tf_op jit(solution)/shard_map/all_gather | solution.py:45
  67.8 3.4 %fusion.3 = bf16[512,256]{1,0:T(8,128)(2,1)S(1)} fusion(bf16[4096,256]{1,0:T(8,128)(2,1)S(1)} %bitcast.27, bf16[1,512,4096]{2,1,0:T(8,128)(2,1)} %all-gather.12.cloned.1.call-done), kind=kOutput, calls=%fused_computation.4 | convolution fusion | flops 1073872896 | bytes 6553600 | tf_op jit(solution)/shard_map/dot_general | solution.py:37
  71.2 1.5 broadcast_in_dim.17
  72.7 4.9 %all-to-all-start.1 = ((bf16[8,512,256]{2,1,0:T(8,128)(2,1)}), bf16[8,512,256]{2,1,0:T(8,128)(2,1)S(1)}, u32[]{:S(2)}, u32[]{:S(2)}) async-start(bf16[8,512,256]{2,1,0:T(8,128)(2,1)} %broadcast_in_dim.17), calls=%async_computation.1 | async-start | bytes 4194304 | tf_op jit(solution)/shard_map/all_to_all | solution.py:25
  77.6 0.0 all-gather.8.cloned.1.call-start
  77.7 45.4 %all-gather.6.cloned.1.call-done = bf16[512,4096]{1,0:T(8,128)(2,1)} async-done(((bf16[512,512]{1,0:T(8,128)(2,1)}), bf16[512,4096]{1,0:T(8,128)(2,1)}) %all-gather.6.cloned.1.call-update) | async-done | bytes 4194320 | tf_op jit(solution)/shard_map/all_gather | solution.py:47
  123.1 4.2 %fusion.6 = bf16[512,256]{0,1:T(8,128)(2,1)} fusion(bf16[4096,256]{1,0:T(8,128)(2,1)S(1)} %bitcast.25, bf16[512,4096]{1,0:T(8,128)(2,1)} %all-gather.6.cloned.1.call-done), kind=kOutput, calls=%fused_computation.7 | convolution fusion | flops 1073872896 | bytes 6553600 | tf_op jit(solution)/shard_map/dot_general | solution.py:37
  127.3 0.0 all-gather.8.cloned.1.call-update
  127.3 0.0 all-gather.10.cloned.1.call-start
  127.4 0.8 collective-permute-start.8
  128.2 1.5 collective-permute-done.8
  129.7 0.8 copy-done.1
  130.5 0.0 all-gather.10.cloned.1.call-update
  130.5 0.1 collective-permute-start
  130.6 2.7 %collective-permute-start.1 = (bf16[512,512]{1,0:T(8,128)(2,1)S(1)}, bf16[512,512]{1,0:T(8,128)(2,1)S(1)}, u32[]{:S(2)}, u32[]{:S(2)}) collective-permute-start(bf16[512,512]{1,0:T(8,128)(2,1)S(1)} %bitcast.31), channel_id=1, source_target_pairs={{0,7},{1,0},{2,1},{3,2},{4,3},{5,4},{6,5},{7,6},{8,15},{9,8},{10,9... | collective-permute-start | bytes 1572872 | tf_op jit(solution)/shard_map/ppermute | solution.py:59
  133.3 11.7 %collective-permute-done = bf16[512,512]{1,0:T(8,128)(2,1)S(1)} collective-permute-done((bf16[512,512]{1,0:T(8,128)(2,1)S(1)}, bf16[512,512]{1,0:T(8,128)(2,1)S(1)}, u32[]{:S(2)}, u32[]{:S(2)}) %collective-permute-start) | collective-permute-done | bytes 524320 | tf_op jit(solution)/shard_map/ppermute | solution.py:56
  145.0 2.7 %collective-permute-start.3 = (bf16[512,512]{1,0:T(8,128)(2,1)S(1)}, bf16[512,512]{1,0:T(8,128)(2,1)S(1)}, u32[]{:S(2)}, u32[]{:S(2)}) collective-permute-start(bf16[512,512]{1,0:T(8,128)(2,1)S(1)} %collective-permute-done.1), channel_id=1, source_target_pairs={{0,7},{1,0},{2,1},{3,2},{4,3},{5,4},{6,5},{7,6},{8,15},{9,8},{10,9... | collective-permute-start | bytes 1572872 | tf_op jit(solution)/shard_map/ppermute | solution.py:59
  147.6 10.7 %collective-permute-done.2 = bf16[512,512]{1,0:T(8,128)(2,1)S(1)} collective-permute-done((bf16[512,512]{1,0:T(8,128)(2,1)S(1)}, bf16[512,512]{1,0:T(8,128)(2,1)S(1)}, u32[]{:S(2)}, u32[]{:S(2)}) %collective-permute-start.2) | collective-permute-done | bytes 524320 | tf_op jit(solution)/shard_map/ppermute | solution.py:56
  158.4 2.5 %broadcast_in_dim.16 = bf16[512,4096]{1,0:T(8,128)(2,1)} broadcast(bf16[]{:T(256)} %constant.49.clone.1), dimensions={} | broadcast | bytes 4194306 | tf_op jit(solution)/shard_map/broadcast_in_dim | solution.py:52
  160.9 0.9 constant_dynamic-update-slice_fusion.7
  161.8 0.0 collective-permute-done.3
  161.8 2.7 %collective-permute-start.5 = (bf16[512,512]{1,0:T(8,128)(2,1)S(1)}, bf16[512,512]{1,0:T(8,128)(2,1)S(1)}, u32[]{:S(2)}, u32[]{:S(2)}) collective-permute-start(bf16[512,512]{1,0:T(8,128)(2,1)S(1)} %collective-permute-done.3), channel_id=1, source_target_pairs={{0,7},{1,0},{2,1},{3,2},{4,3},{5,4},{6,5},{7,6},{8,15},{9,8},{10,9... | collective-permute-start | bytes 1572872 | tf_op jit(solution)/shard_map/ppermute | solution.py:59
  164.5 0.9 constant_dynamic-update-slice_fusion.6
  165.4 5.6 %collective-permute-done.4 = bf16[512,512]{1,0:T(8,128)(2,1)S(1)} collective-permute-done((bf16[512,512]{1,0:T(8,128)(2,1)S(1)}, bf16[512,512]{1,0:T(8,128)(2,1)S(1)}, u32[]{:S(2)}, u32[]{:S(2)}) %collective-permute-start.4) | collective-permute-done | bytes 524320 | tf_op jit(solution)/shard_map/ppermute | solution.py:56
  171.0 0.0 collective-permute-start.6
  171.0 0.9 constant_dynamic-update-slice_fusion.5
  171.9 0.9 constant_dynamic-update-slice_fusion.4
  172.8 0.9 constant_dynamic-update-slice_fusion.3
  173.7 1.0 constant_dynamic-update-slice_fusion.2
  174.6 0.0 collective-permute-done.5
  174.6 0.8 constant_dynamic-update-slice_fusion.1
  175.5 7.2 %collective-permute-done.6 = bf16[512,512]{1,0:T(8,128)(2,1)S(1)} collective-permute-done((bf16[512,512]{1,0:T(8,128)(2,1)S(1)}, bf16[512,512]{1,0:T(8,128)(2,1)S(1)}, u32[]{:S(2)}, u32[]{:S(2)}) %collective-permute-start.6) | collective-permute-done | bytes 524320 | tf_op jit(solution)/shard_map/ppermute | solution.py:56
  182.7 0.9 constant_dynamic-update-slice_fusion
  183.6 4.1 %fusion.2 = bf16[512,256]{1,0:T(8,128)(2,1)S(1)} fusion(bf16[512,4096]{1,0:T(8,128)(2,1)} %constant_dynamic-update-slice_fusion, bf16[4096,256]{0,1:T(8,128)(2,1)} %all-gather.8.cloned.1.call-done, bf16[512,256]{1,0:T(8,128)(2,1)S(1)} %fusion.3), kind=kOutput, calls=%fused_computation.3 | convolution fusion | flops 1074135040 | bytes 6815744 | tf_op jit(solution)/shard_map/dot_general | solution.py:34
  187.8 1.5 broadcast_in_dim.18
  189.2 5.3 %all-to-all-start.2 = ((bf16[8,512,256]{2,1,0:T(8,128)(2,1)}), bf16[8,512,256]{2,1,0:T(8,128)(2,1)S(1)}, u32[]{:S(2)}, u32[]{:S(2)}) async-start(bf16[8,512,256]{2,1,0:T(8,128)(2,1)} %broadcast_in_dim.18), calls=%async_computation.2 | async-start | bytes 4194304 | tf_op jit(solution)/shard_map/all_to_all | solution.py:25
  194.6 42.0 %all-gather.10.cloned.1.call-done = bf16[512,4096]{1,0:T(8,128)(2,1)} async-done(((bf16[512,512]{1,0:T(8,128)(2,1)}), bf16[512,4096]{1,0:T(8,128)(2,1)}) %all-gather.10.cloned.1.call-update) | async-done | bytes 4194320 | tf_op jit(solution)/shard_map/all_gather | solution.py:70
  236.5 0.0 all-to-all-done.2
  236.5 3.5 %fusion.7 = bf16[1,512,256]{1,2,0:T(8,128)(2,1)S(1)} fusion(bf16[4096,256]{1,0:T(8,128)(2,1)S(1)} %bitcast.26, bf16[512,4096]{1,0:T(8,128)(2,1)} %all-gather.10.cloned.1.call-done), kind=kOutput, calls=%fused_computation.8 | convolution fusion | flops 1073872896 | bytes 6553600 | tf_op jit(solution)/shard_map/dot_general | solution.py:37
  240.0 0.8 copy.4
  (12 shorter events, 0.0 us)
Async XLA Ops:
  6.5 61.3 %all-gather.12.cloned.1.call-start = ((), (), s32[]{:S(2)}) async-start(), calls=%async_computation.6 | async-start | bytes 4718592 | tf_op jit(solution)/shard_map/all_gather | solution.py:45
  7.3 115.8 %all-gather.6.cloned.1.call-start = ((), (), s32[]{:S(2)}) async-start(), calls=%async_computation.3 | async-start | bytes 4718592 | tf_op jit(solution)/shard_map/all_gather | solution.py:47
  7.3 5.1 %collective-permute-start.7 = (bf16[512,512]{1,0:T(8,128)(2,1)}, bf16[512,512]{1,0:T(8,128)(2,1)S(1)}, u32[]{:S(2)}, u32[]{:S(2)}) collective-permute-start(bf16[512,512]{1,0:T(8,128)(2,1)} %bitcast.29), channel_id=1, source_target_pairs={{0,64},{64,0},{128,192},{192,128},{1,65},{65,1},{129,193},{193,129... | collective-permute-start | bytes 1572872 | tf_op jit(solution)/shard_map/ppermute | solution.py:14
  12.4 0.9 copy-start.2
  72.7 50.3 %all-to-all-start.1 = ((bf16[8,512,256]{2,1,0:T(8,128)(2,1)}), bf16[8,512,256]{2,1,0:T(8,128)(2,1)S(1)}, u32[]{:S(2)}, u32[]{:S(2)}) async-start(bf16[8,512,256]{2,1,0:T(8,128)(2,1)} %broadcast_in_dim.17), calls=%async_computation.1 | async-start | bytes 4194304 | tf_op jit(solution)/shard_map/all_to_all | solution.py:25
  77.6 49.8 %copy-start = (bf16[1,512,512]{2,1,0:T(8,128)(2,1)S(1)}, bf16[1,512,512]{2,1,0:T(8,128)(2,1)}, u32[]{:S(2)}) copy-start(bf16[1,512,512]{2,1,0:T(8,128)(2,1)} %param.4) | copy-start | bytes 1572868
  77.6 106.0 %all-gather.8.cloned.1.call-start = ((), (), s32[]{:S(2)}) async-start(), calls=%async_computation.4 | async-start | bytes 2359296 | tf_op jit(solution)/shard_map/all_gather | solution.py:67
  123.1 7.5 %copy-start.3 = (bf16[1,512,512]{2,1,0:T(8,128)(2,1)S(1)}, bf16[1,512,512]{2,1,0:T(8,128)(2,1)}, u32[]{:S(2)}) copy-start(bf16[1,512,512]{2,1,0:T(8,128)(2,1)} %param.3) | copy-start | bytes 1572868
  127.3 109.2 %all-gather.10.cloned.1.call-start = ((), (), s32[]{:S(2)}) async-start(), calls=%async_computation.5 | async-start | bytes 4718592 | tf_op jit(solution)/shard_map/all_gather | solution.py:70
  127.4 2.3 collective-permute-start.8
  129.7 0.8 copy-start.1
  130.5 14.4 %collective-permute-start = (bf16[512,512]{1,0:T(8,128)(2,1)S(1)}, bf16[512,512]{1,0:T(8,128)(2,1)S(1)}, u32[]{:S(2)}, u32[]{:S(2)}) collective-permute-start(bf16[512,512]{1,0:T(8,128)(2,1)S(1)} %bitcast.30), channel_id=1, source_target_pairs={{0,1},{1,2},{2,3},{3,4},{4,5},{5,6},{6,7},{7,0},{8,9},{9,10},{10,1... | collective-permute-start | bytes 1572872 | tf_op jit(solution)/shard_map/ppermute | solution.py:56
  130.6 14.3 %collective-permute-start.1 = (bf16[512,512]{1,0:T(8,128)(2,1)S(1)}, bf16[512,512]{1,0:T(8,128)(2,1)S(1)}, u32[]{:S(2)}, u32[]{:S(2)}) collective-permute-start(bf16[512,512]{1,0:T(8,128)(2,1)S(1)} %bitcast.31), channel_id=1, source_target_pairs={{0,7},{1,0},{2,1},{3,2},{4,3},{5,4},{6,5},{7,6},{8,15},{9,8},{10,9... | collective-permute-start | bytes 1572872 | tf_op jit(solution)/shard_map/ppermute | solution.py:59
  145.0 13.4 %collective-permute-start.2 = (bf16[512,512]{1,0:T(8,128)(2,1)S(1)}, bf16[512,512]{1,0:T(8,128)(2,1)S(1)}, u32[]{:S(2)}, u32[]{:S(2)}) collective-permute-start(bf16[512,512]{1,0:T(8,128)(2,1)S(1)} %collective-permute-done), channel_id=1, source_target_pairs={{0,1},{1,2},{2,3},{3,4},{4,5},{5,6},{6,7},{7,0},{8,9},{9,10},{10,1... | collective-permute-start | bytes 1572872 | tf_op jit(solution)/shard_map/ppermute | solution.py:56
  145.0 16.9 %collective-permute-start.3 = (bf16[512,512]{1,0:T(8,128)(2,1)S(1)}, bf16[512,512]{1,0:T(8,128)(2,1)S(1)}, u32[]{:S(2)}, u32[]{:S(2)}) collective-permute-start(bf16[512,512]{1,0:T(8,128)(2,1)S(1)} %collective-permute-done.1), channel_id=1, source_target_pairs={{0,7},{1,0},{2,1},{3,2},{4,3},{5,4},{6,5},{7,6},{8,15},{9,8},{10,9... | collective-permute-start | bytes 1572872 | tf_op jit(solution)/shard_map/ppermute | solution.py:59
  158.4 12.6 %collective-permute-start.4 = (bf16[512,512]{1,0:T(8,128)(2,1)S(1)}, bf16[512,512]{1,0:T(8,128)(2,1)S(1)}, u32[]{:S(2)}, u32[]{:S(2)}) collective-permute-start(bf16[512,512]{1,0:T(8,128)(2,1)S(1)} %collective-permute-done.2), channel_id=1, source_target_pairs={{0,1},{1,2},{2,3},{3,4},{4,5},{5,6},{6,7},{7,0},{8,9},{9,10},{10,1... | collective-permute-start | bytes 1572872 | tf_op jit(solution)/shard_map/ppermute | solution.py:56
  161.8 12.8 %collective-permute-start.5 = (bf16[512,512]{1,0:T(8,128)(2,1)S(1)}, bf16[512,512]{1,0:T(8,128)(2,1)S(1)}, u32[]{:S(2)}, u32[]{:S(2)}) collective-permute-start(bf16[512,512]{1,0:T(8,128)(2,1)S(1)} %collective-permute-done.3), channel_id=1, source_target_pairs={{0,7},{1,0},{2,1},{3,2},{4,3},{5,4},{6,5},{7,6},{8,15},{9,8},{10,9... | collective-permute-start | bytes 1572872 | tf_op jit(solution)/shard_map/ppermute | solution.py:59
  171.0 11.7 %collective-permute-start.6 = (bf16[512,512]{1,0:T(8,128)(2,1)S(1)}, bf16[512,512]{1,0:T(8,128)(2,1)S(1)}, u32[]{:S(2)}, u32[]{:S(2)}) collective-permute-start(bf16[512,512]{1,0:T(8,128)(2,1)S(1)} %collective-permute-done.4), channel_id=1, source_target_pairs={{0,1},{1,2},{2,3},{3,4},{4,5},{5,6},{6,7},{7,0},{8,9},{9,10},{10,1... | collective-permute-start | bytes 1572872 | tf_op jit(solution)/shard_map/ppermute | solution.py:56
  189.2 47.3 %all-to-all-start.2 = ((bf16[8,512,256]{2,1,0:T(8,128)(2,1)}), bf16[8,512,256]{2,1,0:T(8,128)(2,1)S(1)}, u32[]{:S(2)}, u32[]{:S(2)}) async-start(bf16[8,512,256]{2,1,0:T(8,128)(2,1)} %broadcast_in_dim.18), calls=%async_computation.2 | async-start | bytes 4194304 | tf_op jit(solution)/shard_map/all_to_all | solution.py:25
Sparse Core Ops, SparseCore 0:
  9.1 58.6 all-gather.11
  69.6 53.4 all-gather.5
  127.5 51.0 all-gather.7
  180.2 56.3 all-gather.9
